TPU v7x, 32 devices: a whole 2x2x4 slice. The times are simulated.
32 devices in a mesh: sky: 8 (over z, x), tm: 4 (over y, core).
Axes of the slice: x: 2, y: 2, z: 4, core: 2. Of those that a mesh axis runs over, the one named last changes fastest.
Arguments:
- observed: float32 [4096, 128], P(('sky', 'tm')), may hold values from -12 to 12
- att_partials: bfloat16 [3, 4096, 128], P(None, ('sky', 'tm')), may hold values from -6 to 6
- src_partials: bfloat16 [5, 4096, 128], P(None, ('sky', 'tm')), may hold values from -6 to 6
- src_slot: int32 [4096], P(('sky', 'tm')), may hold values from 0 to 1023
- knot_block: int32 [4096], P(('sky', 'tm')), may hold values from 0 to 255, as said below
- live_count: int32 [32], P(('sky', 'tm')), may hold values from 32 to 128, as said below
- sources: float32 [5, 8192], P(None, 'sky'), may hold values from -6 to 6
- inverses: float32 [5, 5, 8192], P(None, None, 'sky')
- attitude: float32 [3, 4, 4096], P(None, 'tm', 'sky'), may hold values from -6 to 6
- band_coef: float32 [3, 3, 4, 4096], P(None, None, 'tm', 'sky'), may hold values from 0.5 to 4
- extra_diag: float32 [3, 4, 4096], P(None, 'tm', 'sky'), may hold values from 0.05 to 0.5
- band_offsets: int32 [3], replicated, may hold values from 1 to 16, as said below
Outputs:
- sources_out: float32 [5, 8192], P(None, 'sky')
- attitude_out: float32 [3, 4, 4096], P(None, 'tm', 'sky')
Inputs may be any that keep to these rules, and one draw needn't show every extreme that they name: On every device, the crossings name blocks of one holder (knot_block // 32) at most 32 times, and some holder exactly 32 times; dead crossings carry blocks too. `live_count`: some device uses all its crossings. `band_offsets`: Distinct; one of them is 16.
All inputs are finite; a program needn't handle non-finite values.
Results may differ from a plain program's by a relative error of at most 0.0003.
Values sent between devices are 32-bit elements; how exact they have to be, the bound alone decides.
A program may use at most 64 MiB of HBM per device.

v0:
```python
import jax
import jax.numpy as jnp
from jax import lax
from jax.sharding import PartitionSpec as P

ROWS = 128
BLOCK_KNOTS = 16
HW = 16
SWEEPS = 3
ITERS = 2


def padded_2(block, sides, width):
    for axis, dim in sides:
        count = lax.axis_size(axis)
        forward = [(i, i + 1) for i in range(count - 1)]
        forward.append((count - 1, 0))
        backward = [(target, source) for source, target in forward]
        low = lax.ppermute(
            lax.slice_in_dim(block, block.shape[dim] - width, None, axis=dim), axis, forward
        )
        high = lax.ppermute(lax.slice_in_dim(block, 0, width, axis=dim), axis, backward)
        block = jnp.concatenate([low, block, high], axis=dim)
    return block


def from_behind(value, axis, steps):
    count = lax.axis_size(axis)
    initial, last = (max(0, -steps), min(count, count - steps))
    return lax.ppermute(value, axis, [(source, source + steps) for source in range(initial, last)])


def spline_table():
    rows_pos = jnp.arange(ROWS, dtype=jnp.float32)
    moments = 1.5 + (BLOCK_KNOTS - 3) * (rows_pos + 0.5) / ROWS
    knot_pos = jnp.arange(BLOCK_KNOTS, dtype=jnp.float32)
    dist = jnp.abs(moments[:, None] - knot_pos[None, :])
    inner = 2.0 / 3.0 - dist * dist + 0.5 * dist * dist * dist
    rest = 2.0 - dist
    outer = rest * rest * rest / 6.0
    return jnp.where(dist < 1.0, inner, jnp.where(dist < 2.0, outer, 0.0))


def source_term(src_partials, values):
    total = jnp.zeros(src_partials.shape[1:], jnp.float32)
    for component in range(5):
        total = total + src_partials[component].astype(jnp.float32) * values[component][:, None]
    return total


def neighbour_sum(field, band_terms, band_offsets, base, length):
    total = jnp.zeros(band_terms.shape[1:], jnp.float32)
    for band_index in range(band_terms.shape[0]):
        offset = band_offsets[band_index]
        upper = lax.dynamic_slice_in_dim(field, base + offset, length, 1)
        lower = lax.dynamic_slice_in_dim(field, base - offset, length, 1)
        total = total + band_terms[band_index] * (upper + lower)
    return total


def extend(field, width):
    padded = padded_2(field, (("sky", 1),), width)
    inner_end = padded.shape[1] - width
    left_rim = padded[:, :width]
    right_rim = padded[:, inner_end:]
    from_before = from_behind(left_rim, "tm", 1)
    from_after = from_behind(right_rim, "tm", -1)
    position = lax.axis_index("sky")
    left_rim = jnp.where(position == 0, from_before, left_rim)
    right_rim = jnp.where(position == lax.axis_size("sky") - 1, from_after, right_rim)
    return jnp.concatenate([left_rim, padded[:, width:inner_end], right_rim], axis=1)


def per_device(
    observed,
    att_partials,
    src_partials,
    src_slot,
    knot_block,
    live_count,
    sources,
    inverses,
    attitude,
    band_coef,
    extra_diag,
    band_offsets,
):
    spline = spline_table()
    crossings_here = observed.shape[0]
    knots_here = attitude.shape[2]
    blocks_here = knots_here // BLOCK_KNOTS
    sky_count = lax.axis_size("sky")
    capacity = 2 * crossings_here // sky_count
    slots_total = sky_count * capacity
    live_rows = (jnp.arange(crossings_here, dtype=jnp.int32) < live_count[0]).astype(jnp.float32)[
        :, None
    ]
    band_terms = band_coef[:, :, 0, :]
    extra_terms = extra_diag[:, 0, :]
    diagonal = extra_terms + 2.0 * jnp.sum(band_terms, axis=0)
    knots_now = attitude[:, 0, :]
    sources_now = sources
    holder = knot_block // blocks_here
    local_block = knot_block % blocks_here
    matches = (holder[:, None] == jnp.arange(sky_count, dtype=jnp.int32)[None, :]).astype(jnp.int32)
    earlier = jnp.cumsum(matches, axis=0) - matches
    column = holder * capacity + jnp.sum(earlier * matches, axis=1)
    asked = jnp.full((slots_total,), blocks_here, jnp.int32).at[column].set(local_block)
    wanted = lax.all_to_all(asked, "sky", split_axis=0, concat_axis=0, tiled=True)
    for outer_step in range(ITERS):
        spare = jnp.zeros((3, 1, BLOCK_KNOTS), jnp.float32)
        own_blocks = jnp.concatenate(
            [knots_now.reshape(3, blocks_here, BLOCK_KNOTS), spare], axis=1
        )
        served = jnp.take(jnp.transpose(own_blocks, (0, 2, 1)), wanted, axis=2)
        arrived = lax.all_to_all(served, "sky", split_axis=2, concat_axis=2, tiled=True)
        fetched = jnp.transpose(jnp.take(arrived, column, axis=2), (0, 2, 1))
        att_term = jnp.zeros(observed.shape, jnp.float32)
        for axis_index in range(3):
            att_term = att_term + att_partials[axis_index].astype(jnp.float32) * jnp.dot(
                fetched[axis_index], spline.T, precision=lax.Precision.HIGHEST
            )
        src_values = jnp.take(sources_now, src_slot, axis=1)
        resid = (observed - source_term(src_partials, src_values) - att_term) * live_rows
        rhs = jnp.stack(
            [
                jnp.sum(src_partials[component].astype(jnp.float32) * resid, axis=1)
                for component in range(5)
            ]
        )
        local_normal = jnp.zeros(sources_now.shape, jnp.float32).at[:, src_slot].add(rhs)
        normal = lax.psum(local_normal, "tm")
        step = jnp.einsum("klm,lm->km", inverses, normal, precision=lax.Precision.HIGHEST)
        sources_now = sources_now + step
        resid = resid - live_rows * source_term(src_partials, jnp.take(step, src_slot, axis=1))
        grads = jnp.stack(
            [
                jnp.dot(
                    att_partials[axis_index].astype(jnp.float32) * resid,
                    spline,
                    precision=lax.Precision.HIGHEST,
                )
                for axis_index in range(3)
            ]
        )
        outgoing = (
            jnp.zeros((3, BLOCK_KNOTS, slots_total), jnp.float32)
            .at[:, :, column]
            .set(jnp.transpose(grads, (0, 2, 1)))
        )
        returned = lax.all_to_all(outgoing, "sky", split_axis=2, concat_axis=2, tiled=True)
        summed = (
            jnp.zeros((3, BLOCK_KNOTS, blocks_here + 1), jnp.float32).at[:, :, wanted].add(returned)
        )
        knot_grad = jnp.transpose(summed[:, :, :blocks_here], (0, 2, 1)).reshape(3, knots_here)
        delta = knot_grad / diagonal
        for sweep_index in range(SWEEPS - 1):
            widened = extend(delta, HW)
            delta = (
                knot_grad + neighbour_sum(widened, band_terms, band_offsets, HW, knots_here)
            ) / diagonal
        knots_now = knots_now + delta
    return (sources_now, knots_now[:, None, :])


def solution(mesh):
    placed = (
        P(("sky", "tm"), None),
        P(None, ("sky", "tm"), None),
        P(None, ("sky", "tm"), None),
        P(("sky", "tm")),
        P(("sky", "tm")),
        P(("sky", "tm")),
        P(None, "sky"),
        P(None, None, "sky"),
        P(None, "tm", "sky"),
        P(None, None, "tm", "sky"),
        P(None, "tm", "sky"),
        P(),
    )
    return jax.shard_map(
        per_device,
        mesh=mesh,
        in_specs=placed,
        out_specs=(P(None, "sky"), P(None, "tm", "sky")),
        check_vma=False,
    )
```

profile of v0, /device:TPU:1, one launch (start us, length us, event | category | flops | bytes accessed | tf_op | source)
XLA Modules:
  0.0 230.4 jit_solution(7839276913477497021)
XLA Ops:
  3.4 6.3 %all-to-all-start = ((s32[8,32,1]{1,2,0:T(1,128)}), s32[8,32,1]{1,2,0:T(1,128)S(1)}, u32[]{:S(2)}, u32[]{:S(2)}) async-start(s32[8,32,1]{1,2,0:T(1,128)} %bitcast.8), calls=%async_computation | async-start | bytes 8192 | tf_op jit(solution)/shard_map/all_to_all | solution.py:109
  27.4 3.6 %copy.86 = f32[5,5,1024]{0,1,2:T(8,128)} copy(f32[5,5,1024]{2,1,0:T(8,128)} %param.25) | data formatting | bytes 204800 | tf_op args[7]
  34.7 5.4 %all-to-all-start.1 = ((f32[8,1,1536]{2,1,0:T(1,128)}), f32[8,1,1536]{2,1,0:T(1,128)S(1)}, u32[]{:S(2)}, u32[]{:S(2)}) async-start(f32[8,1,1536]{2,1,0:T(1,128)} %reshape.339), calls=%async_computation.1 | async-start | bytes 98304 | tf_op jit(solution)/shard_map/all_to_all | solution.py:116
  40.2 5.6 %all-to-all-done.1 = f32[8,1,1536]{2,1,0:T(1,128)S(1)} async-done(((f32[8,1,1536]{2,1,0:T(1,128)}), f32[8,1,1536]{2,1,0:T(1,128)S(1)}, u32[]{:S(2)}, u32[]{:S(2)}) %all-to-all-start.1) | async-done | bytes 49184 | tf_op jit(solution)/shard_map/all_to_all | solution.py:116
  50.7 18.4 %psum.14 = f32[5,1024]{0,1:T(8,128)S(1)} all-reduce(f32[5,1024]{0,1:T(8,128)S(1)} %scatter_custom_fusion.1), channel_id=1, replica_groups=mesh['sky'=8,'tm'=4] {'tm'}, use_global_device_ids=true, to_apply=%region_9.13 | all-reduce | flops 5120 | bytes 40960 | tf_op jit(solution)/shard_map/psum | solution.py:132
  69.1 8.5 %fusion.185 = f32[1024,1,5]{2,1,0:T(1,128)S(1)} fusion(f32[5,1024,1]{0,2,1:T(1,128)S(1)} %bitcast.304, f32[5,5,1024]{0,1,2:T(8,128)} %copy.86), kind=kOutput, calls=%fused_computation.312 | convolution fusion | flops 307200 | bytes 143360 | tf_op jit(solution)/shard_map/klm,lm->km/dot_general | solution.py:133
  80.7 4.3 %scatter_fusion = f32[3,16,256]{1,0,2:T(4,128)S(1)} fusion(f32[3,16,256]{1,0,2:T(4,128)S(1)} %broadcast.97.clone, s32[128]{0:T(128)S(1)} %get-tuple-element.44, f32[128,3,16]{2,1,0:T(4,128)S(1)} %copy.74), kind=kCustom, calls=%fused_computation.10 | custom fusion | bytes 74240 | tf_op jit(solution)/shard_map/scatter | solution.py:149
  86.0 3.5 %all-to-all-start.2 = ((f32[8,1,1536]{2,1,0:T(1,128)}), f32[8,1,1536]{2,1,0:T(1,128)S(1)}, u32[]{:S(2)}, u32[]{:S(2)}) async-start(f32[8,1,1536]{2,1,0:T(1,128)} %reshape.341), calls=%async_computation.2 | async-start | bytes 98304 | tf_op jit(solution)/shard_map/all_to_all | solution.py:151
  89.6 5.6 %all-to-all-done.2 = f32[8,1,1536]{2,1,0:T(1,128)S(1)} async-done(((f32[8,1,1536]{2,1,0:T(1,128)}), f32[8,1,1536]{2,1,0:T(1,128)S(1)}, u32[]{:S(2)}, u32[]{:S(2)}) %all-to-all-start.2) | async-done | bytes 49184 | tf_op jit(solution)/shard_map/all_to_all | solution.py:151
  96.4 8.8 %scatter_fusion.1 = f32[3,16,33]{1,0,2:T(4,128)S(1)} fusion(f32[3,16,33]{1,0,2:T(4,128)S(1)} %broadcast.94.clone, s32[256]{0:T(256)S(1)} %bitcast.316, f32[256,3,16]{2,1,0:T(4,128)S(1)} %bitcast_bitcast_fusion.1), kind=kCustom, calls=%fused_computation.11 | custom fusion | flops 12288 | bytes 148480 | tf_op jit(solution)/shard_map/scatter-add | solution.py:153
  105.7 3.9 %collective-permute-start.2 = (f32[3,16]{1,0:T(4,128)S(1)}, f32[3,16]{1,0:T(4,128)S(1)}, u32[]{:S(2)}, u32[]{:S(2)}) collective-permute-start(f32[3,16]{1,0:T(4,128)S(1)} %get-tuple-element.69), channel_id=1, source_target_pairs={{4,0},{8,4},{12,8},{16,12},{20,16},{24,20},{28,24},{0,28},{5,1},{9... | collective-permute-start | bytes 584 | tf_op jit(solution)/shard_map/ppermute | solution.py:22
  110.6 5.5 %collective-permute-start.1 = (f32[3,16]{1,0:T(4,128)S(1)}, f32[3,16]{1,0:T(4,128)S(1)}, u32[]{:S(2)}, u32[]{:S(2)}) collective-permute-start(f32[3,16]{1,0:T(4,128)S(1)} %collective-permute-done), channel_id=1, source_target_pairs={{0,1},{1,2},{2,3},{4,5},{5,6},{6,7},{8,9},{9,10},{10,11},{12,13},{... | collective-permute-start | bytes 584 | tf_op jit(solution)/shard_map/ppermute | solution.py:30
  121.3 4.2 %collective-permute-start.6 = (f32[3,16]{1,0:T(4,128)S(1)}, f32[3,16]{1,0:T(4,128)S(1)}, u32[]{:S(2)}, u32[]{:S(2)}) collective-permute-start(f32[3,16]{1,0:T(4,128)S(1)} %get-tuple-element.67), channel_id=1, source_target_pairs={{4,0},{8,4},{12,8},{16,12},{20,16},{24,20},{28,24},{0,28},{5,1},{9... | collective-permute-start | bytes 584 | tf_op jit(solution)/shard_map/ppermute | solution.py:22
  126.4 3.1 %collective-permute-start.5 = (f32[3,16]{1,0:T(4,128)S(1)}, f32[3,16]{1,0:T(4,128)S(1)}, u32[]{:S(2)}, u32[]{:S(2)}) collective-permute-start(f32[3,16]{1,0:T(4,128)S(1)} %collective-permute-done.4), channel_id=1, source_target_pairs={{0,1},{1,2},{2,3},{4,5},{5,6},{6,7},{8,9},{9,10},{10,11},{12,13},{... | collective-permute-start | bytes 584 | tf_op jit(solution)/shard_map/ppermute | solution.py:30
  137.1 3.3 %all-to-all-start.3 = ((f32[8,1,1536]{2,1,0:T(1,128)}), f32[8,1,1536]{2,1,0:T(1,128)S(1)}, u32[]{:S(2)}, u32[]{:S(2)}) async-start(f32[8,1,1536]{2,1,0:T(1,128)} %reshape.343), calls=%async_computation.3 | async-start | bytes 98304 | tf_op jit(solution)/shard_map/all_to_all | solution.py:116
  140.7 5.3 %all-to-all-done.3 = f32[8,1,1536]{2,1,0:T(1,128)S(1)} async-done(((f32[8,1,1536]{2,1,0:T(1,128)}), f32[8,1,1536]{2,1,0:T(1,128)S(1)}, u32[]{:S(2)}, u32[]{:S(2)}) %all-to-all-start.3) | async-done | bytes 49184 | tf_op jit(solution)/shard_map/all_to_all | solution.py:116
  150.5 15.7 %psum.15 = f32[5,1024]{0,1:T(8,128)S(1)} all-reduce(f32[5,1024]{0,1:T(8,128)S(1)} %scatter_custom_fusion.4), channel_id=1, replica_groups=mesh['sky'=8,'tm'=4] {'tm'}, use_global_device_ids=true, to_apply=%region_19.23 | all-reduce | flops 5120 | bytes 40960 | tf_op jit(solution)/shard_map/psum | solution.py:132
  166.2 8.5 %fusion.186 = f32[1024,1,5]{2,1,0:T(1,128)S(1)} fusion(f32[5,1024,1]{0,2,1:T(1,128)S(1)} %bitcast.303, f32[5,5,1024]{0,1,2:T(8,128)} %copy.86), kind=kOutput, calls=%fused_computation.313 | convolution fusion | flops 307200 | bytes 143360 | tf_op jit(solution)/shard_map/klm,lm->km/dot_general | solution.py:133
  177.0 4.3 %scatter_fusion.2 = f32[3,16,256]{1,0,2:T(4,128)S(1)} fusion(f32[3,16,256]{1,0,2:T(4,128)S(1)} %broadcast.97, s32[128]{0:T(128)S(1)} %get-tuple-element.44, f32[128,3,16]{2,1,0:T(4,128)S(1)} %copy.81), kind=kCustom, calls=%fused_computation.13 | custom fusion | bytes 74240 | tf_op jit(solution)/shard_map/scatter | solution.py:149
  181.7 8.1 %all_to_all.35 = f32[8,1,1536]{2,1,0:T(1,128)S(1)} all-to-all(f32[8,1,1536]{2,1,0:T(1,128)S(1)} %reshape.345), channel_id=1, replica_groups=mesh['sky'=8,'tm'=4] {'sky'}, dimensions={0} | all-to-all | bytes 98304 | tf_op jit(solution)/shard_map/all_to_all | solution.py:151
  191.0 8.8 %scatter_fusion.3 = f32[3,16,33]{1,0,2:T(4,128)S(1)} fusion(f32[3,16,33]{1,0,2:T(4,128)S(1)} %broadcast.94, s32[256]{0:T(256)S(1)} %bitcast.317, f32[256,3,16]{2,1,0:T(4,128)S(1)} %bitcast_bitcast_fusion), kind=kCustom, calls=%fused_computation.14 | custom fusion | flops 12288 | bytes 148480 | tf_op jit(solution)/shard_map/scatter-add | solution.py:153
  200.2 4.0 %collective-permute-start.10 = (f32[3,16]{1,0:T(4,128)S(1)}, f32[3,16]{1,0:T(4,128)S(1)}, u32[]{:S(2)}, u32[]{:S(2)}) collective-permute-start(f32[3,16]{1,0:T(4,128)S(1)} %get-tuple-element.65), channel_id=1, source_target_pairs={{4,0},{8,4},{12,8},{16,12},{20,16},{24,20},{28,24},{0,28},{5,1},{9... | collective-permute-start | bytes 584 | tf_op jit(solution)/shard_map/ppermute | solution.py:22
  205.2 5.4 %collective-permute-start.9 = (f32[3,16]{1,0:T(4,128)S(1)}, f32[3,16]{1,0:T(4,128)S(1)}, u32[]{:S(2)}, u32[]{:S(2)}) collective-permute-start(f32[3,16]{1,0:T(4,128)S(1)} %collective-permute-done.8), channel_id=1, source_target_pairs={{0,1},{1,2},{2,3},{4,5},{5,6},{6,7},{8,9},{9,10},{10,11},{12,13},{... | collective-permute-start | bytes 584 | tf_op jit(solution)/shard_map/ppermute | solution.py:30
  215.8 4.2 %collective-permute-start.14 = (f32[3,16]{1,0:T(4,128)S(1)}, f32[3,16]{1,0:T(4,128)S(1)}, u32[]{:S(2)}, u32[]{:S(2)}) collective-permute-start(f32[3,16]{1,0:T(4,128)S(1)} %get-tuple-element.63), channel_id=1, source_target_pairs={{4,0},{8,4},{12,8},{16,12},{20,16},{24,20},{28,24},{0,28},{5,1},{9... | collective-permute-start | bytes 584 | tf_op jit(solution)/shard_map/ppermute | solution.py:22
  (170 shorter events, 66.2 us)
Async XLA Ops:
  0.6 30.3 %copy-start = (f32[3,3,1,512]{3,2,1,0:T(1,128)S(1)}, f32[3,3,1,512]{3,2,1,0:T(1,128)}, u32[]{:S(2)}) copy-start(f32[3,3,1,512]{3,2,1,0:T(1,128)} %param.27) | copy-start | bytes 55300
  3.4 27.6 %all-to-all-start = ((s32[8,32,1]{1,2,0:T(1,128)}), s32[8,32,1]{1,2,0:T(1,128)S(1)}, u32[]{:S(2)}, u32[]{:S(2)}) async-start(s32[8,32,1]{1,2,0:T(1,128)} %bitcast.8), calls=%async_computation | async-start | bytes 8192 | tf_op jit(solution)/shard_map/all_to_all | solution.py:109
  34.7 11.1 %all-to-all-start.1 = ((f32[8,1,1536]{2,1,0:T(1,128)}), f32[8,1,1536]{2,1,0:T(1,128)S(1)}, u32[]{:S(2)}, u32[]{:S(2)}) async-start(f32[8,1,1536]{2,1,0:T(1,128)} %reshape.339), calls=%async_computation.1 | async-start | bytes 98304 | tf_op jit(solution)/shard_map/all_to_all | solution.py:116
  77.7 27.7 %copy-start.2 = (f32[3,1,512]{2,1,0:T(1,128)S(1)}, f32[3,1,512]{2,1,0:T(1,128)}, u32[]{:S(2)}) copy-start(f32[3,1,512]{2,1,0:T(1,128)} %param.28) | copy-start | bytes 18436
  77.7 56.8 %copy-start.1 = (f32[3,1,512]{2,1,0:T(1,128)S(1)}, f32[3,1,512]{2,1,0:T(1,128)}, u32[]{:S(2)}) copy-start(f32[3,1,512]{2,1,0:T(1,128)} %param.26) | copy-start | bytes 18436
  86.0 9.1 %all-to-all-start.2 = ((f32[8,1,1536]{2,1,0:T(1,128)}), f32[8,1,1536]{2,1,0:T(1,128)S(1)}, u32[]{:S(2)}, u32[]{:S(2)}) async-start(f32[8,1,1536]{2,1,0:T(1,128)} %reshape.341), calls=%async_computation.2 | async-start | bytes 98304 | tf_op jit(solution)/shard_map/all_to_all | solution.py:151
  105.4 5.1 %collective-permute-start = (f32[3,16]{1,0:T(4,128)S(1)}, f32[3,16]{1,0:T(4,128)S(1)}, u32[]{:S(2)}, u32[]{:S(2)}) collective-permute-start(f32[3,16]{1,0:T(4,128)S(1)} %get-tuple-element.68), channel_id=1, source_target_pairs={{0,4},{4,8},{8,12},{12,16},{16,20},{20,24},{24,28},{28,0},{1,5},{5... | collective-permute-start | bytes 584 | tf_op jit(solution)/shard_map/ppermute | solution.py:19
  105.7 10.4 %collective-permute-start.2 = (f32[3,16]{1,0:T(4,128)S(1)}, f32[3,16]{1,0:T(4,128)S(1)}, u32[]{:S(2)}, u32[]{:S(2)}) collective-permute-start(f32[3,16]{1,0:T(4,128)S(1)} %get-tuple-element.69), channel_id=1, source_target_pairs={{4,0},{8,4},{12,8},{16,12},{20,16},{24,20},{28,24},{0,28},{5,1},{9... | collective-permute-start | bytes 584 | tf_op jit(solution)/shard_map/ppermute | solution.py:22
  110.6 7.5 %collective-permute-start.1 = (f32[3,16]{1,0:T(4,128)S(1)}, f32[3,16]{1,0:T(4,128)S(1)}, u32[]{:S(2)}, u32[]{:S(2)}) collective-permute-start(f32[3,16]{1,0:T(4,128)S(1)} %collective-permute-done), channel_id=1, source_target_pairs={{0,1},{1,2},{2,3},{4,5},{5,6},{6,7},{8,9},{9,10},{10,11},{12,13},{... | collective-permute-start | bytes 584 | tf_op jit(solution)/shard_map/ppermute | solution.py:30
  116.1 4.9 %collective-permute-start.3 = (f32[3,16]{1,0:T(4,128)S(1)}, f32[3,16]{1,0:T(4,128)S(1)}, u32[]{:S(2)}, u32[]{:S(2)}) collective-permute-start(f32[3,16]{1,0:T(4,128)S(1)} %collective-permute-done.2), channel_id=1, source_target_pairs={{1,0},{2,1},{3,2},{5,4},{6,5},{7,6},{9,8},{10,9},{11,10},{13,12},{... | collective-permute-start | bytes 584 | tf_op jit(solution)/shard_map/ppermute | solution.py:30
  121.3 5.1 %collective-permute-start.4 = (f32[3,16]{1,0:T(4,128)S(1)}, f32[3,16]{1,0:T(4,128)S(1)}, u32[]{:S(2)}, u32[]{:S(2)}) collective-permute-start(f32[3,16]{1,0:T(4,128)S(1)} %get-tuple-element.66), channel_id=1, source_target_pairs={{0,4},{4,8},{8,12},{12,16},{16,20},{20,24},{24,28},{28,0},{1,5},{5... | collective-permute-start | bytes 584 | tf_op jit(solution)/shard_map/ppermute | solution.py:19
  121.3 8.2 %collective-permute-start.6 = (f32[3,16]{1,0:T(4,128)S(1)}, f32[3,16]{1,0:T(4,128)S(1)}, u32[]{:S(2)}, u32[]{:S(2)}) collective-permute-start(f32[3,16]{1,0:T(4,128)S(1)} %get-tuple-element.67), channel_id=1, source_target_pairs={{4,0},{8,4},{12,8},{16,12},{20,16},{24,20},{28,24},{0,28},{5,1},{9... | collective-permute-start | bytes 584 | tf_op jit(solution)/shard_map/ppermute | solution.py:22
  126.4 5.0 %collective-permute-start.5 = (f32[3,16]{1,0:T(4,128)S(1)}, f32[3,16]{1,0:T(4,128)S(1)}, u32[]{:S(2)}, u32[]{:S(2)}) collective-permute-start(f32[3,16]{1,0:T(4,128)S(1)} %collective-permute-done.4), channel_id=1, source_target_pairs={{0,1},{1,2},{2,3},{4,5},{5,6},{6,7},{8,9},{9,10},{10,11},{12,13},{... | collective-permute-start | bytes 584 | tf_op jit(solution)/shard_map/ppermute | solution.py:30
  129.5 4.9 %collective-permute-start.7 = (f32[3,16]{1,0:T(4,128)S(1)}, f32[3,16]{1,0:T(4,128)S(1)}, u32[]{:S(2)}, u32[]{:S(2)}) collective-permute-start(f32[3,16]{1,0:T(4,128)S(1)} %collective-permute-done.6), channel_id=1, source_target_pairs={{1,0},{2,1},{3,2},{5,4},{6,5},{7,6},{9,8},{10,9},{11,10},{13,12},{... | collective-permute-start | bytes 584 | tf_op jit(solution)/shard_map/ppermute | solution.py:30
  137.1 8.9 %all-to-all-start.3 = ((f32[8,1,1536]{2,1,0:T(1,128)}), f32[8,1,1536]{2,1,0:T(1,128)S(1)}, u32[]{:S(2)}, u32[]{:S(2)}) async-start(f32[8,1,1536]{2,1,0:T(1,128)} %reshape.343), calls=%async_computation.3 | async-start | bytes 98304 | tf_op jit(solution)/shard_map/all_to_all | solution.py:116
  200.0 5.1 %collective-permute-start.8 = (f32[3,16]{1,0:T(4,128)S(1)}, f32[3,16]{1,0:T(4,128)S(1)}, u32[]{:S(2)}, u32[]{:S(2)}) collective-permute-start(f32[3,16]{1,0:T(4,128)S(1)} %get-tuple-element.64), channel_id=1, source_target_pairs={{0,4},{4,8},{8,12},{12,16},{16,20},{20,24},{24,28},{28,0},{1,5},{5... | collective-permute-start | bytes 584 | tf_op jit(solution)/shard_map/ppermute | solution.py:19
  200.2 10.4 %collective-permute-start.10 = (f32[3,16]{1,0:T(4,128)S(1)}, f32[3,16]{1,0:T(4,128)S(1)}, u32[]{:S(2)}, u32[]{:S(2)}) collective-permute-start(f32[3,16]{1,0:T(4,128)S(1)} %get-tuple-element.65), channel_id=1, source_target_pairs={{4,0},{8,4},{12,8},{16,12},{20,16},{24,20},{28,24},{0,28},{5,1},{9... | collective-permute-start | bytes 584 | tf_op jit(solution)/shard_map/ppermute | solution.py:22
  205.2 7.3 %collective-permute-start.9 = (f32[3,16]{1,0:T(4,128)S(1)}, f32[3,16]{1,0:T(4,128)S(1)}, u32[]{:S(2)}, u32[]{:S(2)}) collective-permute-start(f32[3,16]{1,0:T(4,128)S(1)} %collective-permute-done.8), channel_id=1, source_target_pairs={{0,1},{1,2},{2,3},{4,5},{5,6},{6,7},{8,9},{9,10},{10,11},{12,13},{... | collective-permute-start | bytes 584 | tf_op jit(solution)/shard_map/ppermute | solution.py:30
  210.6 4.9 %collective-permute-start.11 = (f32[3,16]{1,0:T(4,128)S(1)}, f32[3,16]{1,0:T(4,128)S(1)}, u32[]{:S(2)}, u32[]{:S(2)}) collective-permute-start(f32[3,16]{1,0:T(4,128)S(1)} %collective-permute-done.10), channel_id=1, source_target_pairs={{1,0},{2,1},{3,2},{5,4},{6,5},{7,6},{9,8},{10,9},{11,10},{13,12},{... | collective-permute-start | bytes 584 | tf_op jit(solution)/shard_map/ppermute | solution.py:30
  215.7 5.1 %collective-permute-start.12 = (f32[3,16]{1,0:T(4,128)S(1)}, f32[3,16]{1,0:T(4,128)S(1)}, u32[]{:S(2)}, u32[]{:S(2)}) collective-permute-start(f32[3,16]{1,0:T(4,128)S(1)} %get-tuple-element.62), channel_id=1, source_target_pairs={{0,4},{4,8},{8,12},{12,16},{16,20},{20,24},{24,28},{28,0},{1,5},{5... | collective-permute-start | bytes 584 | tf_op jit(solution)/shard_map/ppermute | solution.py:19
  215.8 9.0 %collective-permute-start.14 = (f32[3,16]{1,0:T(4,128)S(1)}, f32[3,16]{1,0:T(4,128)S(1)}, u32[]{:S(2)}, u32[]{:S(2)}) collective-permute-start(f32[3,16]{1,0:T(4,128)S(1)} %get-tuple-element.63), channel_id=1, source_target_pairs={{4,0},{8,4},{12,8},{16,12},{20,16},{24,20},{28,24},{0,28},{5,1},{9... | collective-permute-start | bytes 584 | tf_op jit(solution)/shard_map/ppermute | solution.py:22
  220.9 5.8 %collective-permute-start.13 = (f32[3,16]{1,0:T(4,128)S(1)}, f32[3,16]{1,0:T(4,128)S(1)}, u32[]{:S(2)}, u32[]{:S(2)}) collective-permute-start(f32[3,16]{1,0:T(4,128)S(1)} %collective-permute-done.12), channel_id=1, source_target_pairs={{0,1},{1,2},{2,3},{4,5},{5,6},{6,7},{8,9},{9,10},{10,11},{12,13},{... | collective-permute-start | bytes 584 | tf_op jit(solution)/shard_map/ppermute | solution.py:30
  224.8 4.9 %collective-permute-start.15 = (f32[3,16]{1,0:T(4,128)S(1)}, f32[3,16]{1,0:T(4,128)S(1)}, u32[]{:S(2)}, u32[]{:S(2)}) collective-permute-start(f32[3,16]{1,0:T(4,128)S(1)} %collective-permute-done.14), channel_id=1, source_target_pairs={{1,0},{2,1},{3,2},{5,4},{6,5},{7,6},{9,8},{10,9},{11,10},{13,12},{... | collective-permute-start | bytes 584 | tf_op jit(solution)/shard_map/ppermute | solution.py:30
where the time goes:
time: 232 us; the launch traced here: 230 us
  starting transfers between devices  60.1 us (26%)
  blocking collectives  42.1 us (18%)
  local copies, waits for them, and re-layouts  37 us (16%)
  waiting for transfers between devices  32.1 us (14%)
  other arithmetic  28.5 us (12%)
  matrix products  20.9 us (9%)
  between operations  9.85 us (4%)
    psum x2, blocking collectives, per_device(): normal = lax.psum(local_normal, 'tm')  34 us
    ppermute x8, starting transfers between devices, from_behind(): lax.ppermute(value, axis, [(source, source + steps) for source in range(i...  24.7 us
    scatter-add x2, other arithmetic, per_device(): jnp.zeros((3, BLOCK_KNOTS, blocks_here + 1), jnp.float32).at[:, :, wanted]  17.6 us
    dot_general x2, matrix products, per_device(): jnp.einsum('klm,lm->km', inverses, normal, precision=lax.Precision.HIGHEST)  17.1 us
    ppermute x4, starting transfers between devices, padded_2(): lax.ppermute(lax.slice_in_dim(block, 0, width, axis=dim), axis, backward)  16.3 us
    unnamed x27, local copies, waits for them, and re-layouts  12.5 us
    ppermute x8, waiting for transfers between devices, from_behind(): lax.ppermute(value, axis, [(source, source + steps) for source in range(i...  11.8 us
    all_to_all x2, waiting for transfers between devices, per_device(): lax.all_to_all(served, 'sky', split_axis=2, concat_axis=2, tiled=True)  10.9 us
  transfers between devices with their start and end apart: 20, of which 11 were waited for; matrix products, arithmetic and copies ran while one was open for 6% of the time, Pallas kernels for 0%

commit v1 on v0

--- a/solution.py
+++ b/solution.py
@@ -113,7 +113,31 @@
             [knots_now.reshape(3, blocks_here, BLOCK_KNOTS), spare], axis=1
         )
         served = jnp.take(jnp.transpose(own_blocks, (0, 2, 1)), wanted, axis=2)
-        arrived = lax.all_to_all(served, "sky", split_axis=2, concat_axis=2, tiled=True)
+
+        def packet_take(payload, device_axis):
+            step_out, view_out = (lax.axis_size(device_axis), lax.axis_index(device_axis))
+            base_arr = payload.shape[2] // step_out
+            a_next = list(payload.shape)
+            a_next[2] = base_arr
+            fresh = a_next[2]
+            a_next[2] = fresh * step_out
+            r1 = jnp.zeros(a_next, payload.dtype)
+            num = 0
+            while num < step_out:
+                parts_out = lax.dynamic_slice_in_dim(
+                    payload, (view_out ^ num) * base_arr, base_arr, axis=2
+                )
+                if num:
+                    parts_out = lax.ppermute(
+                        parts_out, device_axis, [(pp, pp ^ num) for pp in range(step_out)]
+                    )
+                r1 = lax.dynamic_update_slice_in_dim(
+                    r1, parts_out, (view_out ^ num) * fresh, axis=2
+                )
+                num += 1
+            return r1
+
+        arrived = packet_take(served, "sky")
         fetched = jnp.transpose(jnp.take(arrived, column, axis=2), (0, 2, 1))
         att_term = jnp.zeros(observed.shape, jnp.float32)
         for axis_index in range(3):

time: 232 us -> 240 us (1.034)
  starting transfers between devices: 60.1 us -> 70.1 us
  blocking collectives: 42.1 us -> 46.5 us
  local copies, waits for them, and re-layouts: 37 us -> 33.3 us
    ppermute x0 -> x14, starting transfers between devices: none -> 18.8 us  [packet_take(): lax.ppermute(parts_out, device_axis, [(pp, pp ^ num) for pp in range(step...]
    all_to_all x2 -> x0, waiting for transfers between devices: 10.9 us -> none  [per_device(): lax.all_to_all(served, 'sky', split_axis=2, concat_axis=2, tiled=True)]
    ppermute x0 -> x14, waiting for transfers between devices: none -> 10.2 us  [packet_take(): lax.ppermute(parts_out, device_axis, [(pp, pp ^ num) for pp in range(step...]
    all_to_all x2 -> x0, starting transfers between devices: 8.78 us -> none  [per_device(): lax.all_to_all(served, 'sky', split_axis=2, concat_axis=2, tiled=True)]
    unnamed x27, local copies, waits for them, and re-layouts: 12.5 us -> 8.17 us
    all_to_all x1, blocking collectives: 8.06 us -> 10.9 us  [per_device(): lax.all_to_all(outgoing, 'sky', split_axis=2, concat_axis=2, tiled=True)]
  transfers between devices with their start and end apart: 20 -> 32, of which waited for: 11 -> 12; matrix products, arithmetic and copies ran while one was open for 6% -> 5% of each run, Pallas kernels for 0% -> 0%
where the time goes in v1:
time: 240 us; the launch traced here: 239 us
  starting transfers between devices  70.1 us (29%)
  blocking collectives  46.5 us (19%)
  local copies, waits for them, and re-layouts  33.3 us (14%)
  waiting for transfers between devices  31.4 us (13%)
  other arithmetic  27 us (11%)
  matrix products  20.9 us (9%)
  between operations  9.71 us (4%)
    psum x2, blocking collectives, per_device(): normal = lax.psum(local_normal, 'tm')  35.6 us
    ppermute x8, starting transfers between devices, from_behind(): lax.ppermute(value, axis, [(source, source + steps) for source in range(i...  24.9 us
    ppermute x14, starting transfers between devices, packet_take(): lax.ppermute(parts_out, device_axis, [(pp, pp ^ num) for pp in range(step...  18.8 us
    scatter-add x2, other arithmetic, per_device(): jnp.zeros((3, BLOCK_KNOTS, blocks_here + 1), jnp.float32).at[:, :, wanted]  17.6 us
    dot_general x2, matrix products, per_device(): jnp.einsum('klm,lm->km', inverses, normal, precision=lax.Precision.HIGHEST)  17.1 us
    ppermute x4, starting transfers between devices, padded_2(): lax.ppermute(lax.slice_in_dim(block, 0, width, axis=dim), axis, backward)  16.6 us
    ppermute x8, waiting for transfers between devices, from_behind(): lax.ppermute(value, axis, [(source, source + steps) for source in range(i...  11.8 us
    all_to_all x1, blocking collectives, per_device(): lax.all_to_all(outgoing, 'sky', split_axis=2, concat_axis=2, tiled=True)  10.9 us
  transfers between devices with their start and end apart: 32, of which 12 were waited for; matrix products, arithmetic and copies ran while one was open for 5% of the time, Pallas kernels for 0%

profile of v1, /device:TPU:1, one launch (start us, length us, event | category | flops | bytes accessed | tf_op | source)
XLA Modules:
  0.0 238.9 jit_solution(16156491564012795584)
XLA Ops:
  3.5 6.3 %all-to-all-start = ((s32[8,32,1]{1,2,0:T(1,128)}), s32[8,32,1]{1,2,0:T(1,128)S(1)}, u32[]{:S(2)}, u32[]{:S(2)}) async-start(s32[8,32,1]{1,2,0:T(1,128)} %bitcast.8), calls=%async_computation | async-start | bytes 8192 | tf_op jit(solution)/shard_map/all_to_all | solution.py:109
  38.3 3.0 %collective-permute-start.5 = (f32[3,16,32]{1,0,2:T(4,128)S(1)}, f32[3,16,32]{1,0,2:T(4,128)S(1)}, u32[]{:S(2)}, u32[]{:S(2)}) collective-permute-start(f32[3,16,32]{1,0,2:T(4,128)S(1)} %get-tuple-element.54), channel_id=1, source_target_pairs={{0,24},{4,28},{8,16},{12,20},{16,8},{20,12},{24,0},{28,4},{1,25},{... | collective-permute-start | bytes 18440 | tf_op jit(solution)/shard_map/ppermute | solution.py:131
  41.6 5.9 %collective-permute-done.4 = f32[3,16,32]{1,0,2:T(4,128)S(1)} collective-permute-done((f32[3,16,32]{1,0,2:T(4,128)S(1)}, f32[3,16,32]{1,0,2:T(4,128)S(1)}, u32[]{:S(2)}, u32[]{:S(2)}) %collective-permute-start.4) | collective-permute-done | bytes 6176 | tf_op jit(solution)/shard_map/ppermute | solution.py:131
  50.9 19.8 %psum.14 = f32[5,1024]{0,1:T(8,128)S(1)} all-reduce(f32[5,1024]{0,1:T(8,128)S(1)} %scatter_custom_fusion.1), channel_id=1, replica_groups=mesh['sky'=8,'tm'=4] {'tm'}, use_global_device_ids=true, to_apply=%region_9.13 | all-reduce | flops 5120 | bytes 40960 | tf_op jit(solution)/shard_map/psum | solution.py:156
  70.7 8.5 %fusion.195 = f32[1024,1,5]{2,1,0:T(1,128)S(1)} fusion(f32[5,1024,1]{0,2,1:T(1,128)S(1)} %bitcast.246, f32[5,5,1024]{0,1,2:T(8,128)} %copy.86), kind=kOutput, calls=%fused_computation.376 | convolution fusion | flops 307200 | bytes 143360 | tf_op jit(solution)/shard_map/klm,lm->km/dot_general | solution.py:157
  82.3 4.3 %scatter_fusion = f32[3,16,256]{1,0,2:T(4,128)S(1)} fusion(f32[3,16,256]{1,0,2:T(4,128)S(1)} %broadcast.93.clone.1, s32[128]{0:T(128)S(1)} %get-tuple-element.44, f32[128,3,16]{2,1,0:T(4,128)S(1)} %copy.74), kind=kCustom, calls=%fused_computation.10 | custom fusion | bytes 74240 | tf_op jit(solution)/shard_map/scatter | solution.py:173
  87.6 3.3 %all-to-all-start.1 = ((f32[8,1,1536]{2,1,0:T(1,128)}), f32[8,1,1536]{2,1,0:T(1,128)S(1)}, u32[]{:S(2)}, u32[]{:S(2)}) async-start(f32[8,1,1536]{2,1,0:T(1,128)} %reshape.339), calls=%async_computation.1 | async-start | bytes 98304 | tf_op jit(solution)/shard_map/all_to_all | solution.py:175
  90.9 5.6 %all-to-all-done.1 = f32[8,1,1536]{2,1,0:T(1,128)S(1)} async-done(((f32[8,1,1536]{2,1,0:T(1,128)}), f32[8,1,1536]{2,1,0:T(1,128)S(1)}, u32[]{:S(2)}, u32[]{:S(2)}) %all-to-all-start.1) | async-done | bytes 49184 | tf_op jit(solution)/shard_map/all_to_all | solution.py:175
  98.2 8.8 %scatter_fusion.1 = f32[3,16,33]{1,0,2:T(4,128)S(1)} fusion(f32[3,16,33]{1,0,2:T(4,128)S(1)} %broadcast.98.clone, s32[256]{0:T(256)S(1)} %bitcast.256, f32[256,3,16]{2,1,0:T(4,128)S(1)} %bitcast_bitcast_fusion.1), kind=kCustom, calls=%fused_computation.11 | custom fusion | flops 12288 | bytes 148480 | tf_op jit(solution)/shard_map/scatter-add | solution.py:177
  107.4 4.1 %collective-permute-start.9 = (f32[3,16]{1,0:T(4,128)S(1)}, f32[3,16]{1,0:T(4,128)S(1)}, u32[]{:S(2)}, u32[]{:S(2)}) collective-permute-start(f32[3,16]{1,0:T(4,128)S(1)} %get-tuple-element.85), channel_id=1, source_target_pairs={{4,0},{8,4},{12,8},{16,12},{20,16},{24,20},{28,24},{0,28},{5,1},{9... | collective-permute-start | bytes 584 | tf_op jit(solution)/shard_map/ppermute | solution.py:22
  112.4 5.6 %collective-permute-start.8 = (f32[3,16]{1,0:T(4,128)S(1)}, f32[3,16]{1,0:T(4,128)S(1)}, u32[]{:S(2)}, u32[]{:S(2)}) collective-permute-start(f32[3,16]{1,0:T(4,128)S(1)} %collective-permute-done.7), channel_id=1, source_target_pairs={{0,1},{1,2},{2,3},{4,5},{5,6},{6,7},{8,9},{9,10},{10,11},{12,13},{... | collective-permute-start | bytes 584 | tf_op jit(solution)/shard_map/ppermute | solution.py:30
  123.2 4.2 %collective-permute-start.13 = (f32[3,16]{1,0:T(4,128)S(1)}, f32[3,16]{1,0:T(4,128)S(1)}, u32[]{:S(2)}, u32[]{:S(2)}) collective-permute-start(f32[3,16]{1,0:T(4,128)S(1)} %get-tuple-element.83), channel_id=1, source_target_pairs={{4,0},{8,4},{12,8},{16,12},{20,16},{24,20},{28,24},{0,28},{5,1},{9... | collective-permute-start | bytes 584 | tf_op jit(solution)/shard_map/ppermute | solution.py:22
  128.4 3.1 %collective-permute-start.12 = (f32[3,16]{1,0:T(4,128)S(1)}, f32[3,16]{1,0:T(4,128)S(1)}, u32[]{:S(2)}, u32[]{:S(2)}) collective-permute-start(f32[3,16]{1,0:T(4,128)S(1)} %collective-permute-done.11), channel_id=1, source_target_pairs={{0,1},{1,2},{2,3},{4,5},{5,6},{6,7},{8,9},{9,10},{10,11},{12,13},{... | collective-permute-start | bytes 584 | tf_op jit(solution)/shard_map/ppermute | solution.py:30
  144.8 3.2 %collective-permute-start.21 = (f32[3,16,32]{1,0,2:T(4,128)S(1)}, f32[3,16,32]{1,0,2:T(4,128)S(1)}, u32[]{:S(2)}, u32[]{:S(2)}) collective-permute-start(f32[3,16,32]{1,0,2:T(4,128)S(1)} %get-tuple-element.45), channel_id=1, source_target_pairs={{0,28},{4,24},{8,20},{12,16},{16,12},{20,8},{24,4},{28,0},{1,29},{... | collective-permute-start | bytes 18440 | tf_op jit(solution)/shard_map/ppermute | solution.py:131
  148.0 3.0 %collective-permute-done.18 = f32[3,16,32]{1,0,2:T(4,128)S(1)} collective-permute-done((f32[3,16,32]{1,0,2:T(4,128)S(1)}, f32[3,16,32]{1,0,2:T(4,128)S(1)}, u32[]{:S(2)}, u32[]{:S(2)}) %collective-permute-start.18) | collective-permute-done | bytes 6176 | tf_op jit(solution)/shard_map/ppermute | solution.py:131
  155.8 15.8 %psum.15 = f32[5,1024]{0,1:T(8,128)S(1)} all-reduce(f32[5,1024]{0,1:T(8,128)S(1)} %scatter_custom_fusion.4), channel_id=1, replica_groups=mesh['sky'=8,'tm'=4] {'tm'}, use_global_device_ids=true, to_apply=%region_19.23 | all-reduce | flops 5120 | bytes 40960 | tf_op jit(solution)/shard_map/psum | solution.py:156
  171.6 8.5 %fusion.196 = f32[1024,1,5]{2,1,0:T(1,128)S(1)} fusion(f32[5,1024,1]{0,2,1:T(1,128)S(1)} %bitcast.245, f32[5,5,1024]{0,1,2:T(8,128)} %copy.86), kind=kOutput, calls=%fused_computation.377 | convolution fusion | flops 307200 | bytes 143360 | tf_op jit(solution)/shard_map/klm,lm->km/dot_general | solution.py:157
  182.5 4.3 %scatter_fusion.2 = f32[3,16,256]{1,0,2:T(4,128)S(1)} fusion(f32[3,16,256]{1,0,2:T(4,128)S(1)} %broadcast.93, s32[128]{0:T(128)S(1)} %get-tuple-element.44, f32[128,3,16]{2,1,0:T(4,128)S(1)} %copy.81), kind=kCustom, calls=%fused_computation.13 | custom fusion | bytes 74240 | tf_op jit(solution)/shard_map/scatter | solution.py:173
  187.2 10.9 %all_to_all.25 = f32[8,1,1536]{2,1,0:T(1,128)S(1)} all-to-all(f32[8,1,1536]{2,1,0:T(1,128)S(1)} %reshape.341), channel_id=1, replica_groups=mesh['sky'=8,'tm'=4] {'sky'}, dimensions={0} | all-to-all | bytes 98304 | tf_op jit(solution)/shard_map/all_to_all | solution.py:175
  199.4 8.8 %scatter_fusion.3 = f32[3,16,33]{1,0,2:T(4,128)S(1)} fusion(f32[3,16,33]{1,0,2:T(4,128)S(1)} %broadcast.98, s32[256]{0:T(256)S(1)} %bitcast.257, f32[256,3,16]{2,1,0:T(4,128)S(1)} %bitcast_bitcast_fusion), kind=kCustom, calls=%fused_computation.14 | custom fusion | flops 12288 | bytes 148480 | tf_op jit(solution)/shard_map/scatter-add | solution.py:177
  208.4 4.2 %collective-permute-start.24 = (f32[3,16]{1,0:T(4,128)S(1)}, f32[3,16]{1,0:T(4,128)S(1)}, u32[]{:S(2)}, u32[]{:S(2)}) collective-permute-start(f32[3,16]{1,0:T(4,128)S(1)} %get-tuple-element.81), channel_id=1, source_target_pairs={{4,0},{8,4},{12,8},{16,12},{20,16},{24,20},{28,24},{0,28},{5,1},{9... | collective-permute-start | bytes 584 | tf_op jit(solution)/shard_map/ppermute | solution.py:22
  213.5 5.5 %collective-permute-start.23 = (f32[3,16]{1,0:T(4,128)S(1)}, f32[3,16]{1,0:T(4,128)S(1)}, u32[]{:S(2)}, u32[]{:S(2)}) collective-permute-start(f32[3,16]{1,0:T(4,128)S(1)} %collective-permute-done.22), channel_id=1, source_target_pairs={{0,1},{1,2},{2,3},{4,5},{5,6},{6,7},{8,9},{9,10},{10,11},{12,13},{... | collective-permute-start | bytes 584 | tf_op jit(solution)/shard_map/ppermute | solution.py:30
  224.2 4.2 %collective-permute-start.28 = (f32[3,16]{1,0:T(4,128)S(1)}, f32[3,16]{1,0:T(4,128)S(1)}, u32[]{:S(2)}, u32[]{:S(2)}) collective-permute-start(f32[3,16]{1,0:T(4,128)S(1)} %get-tuple-element.79), channel_id=1, source_target_pairs={{4,0},{8,4},{12,8},{16,12},{20,16},{24,20},{28,24},{0,28},{5,1},{9... | collective-permute-start | bytes 584 | tf_op jit(solution)/shard_map/ppermute | solution.py:22
  229.3 3.1 %collective-permute-start.27 = (f32[3,16]{1,0:T(4,128)S(1)}, f32[3,16]{1,0:T(4,128)S(1)}, u32[]{:S(2)}, u32[]{:S(2)}) collective-permute-start(f32[3,16]{1,0:T(4,128)S(1)} %collective-permute-done.26), channel_id=1, source_target_pairs={{0,1},{1,2},{2,3},{4,5},{5,6},{6,7},{8,9},{9,10},{10,11},{12,13},{... | collective-permute-start | bytes 584 | tf_op jit(solution)/shard_map/ppermute | solution.py:30
  (210 shorter events, 75.1 us)
Async XLA Ops:
  3.5 14.4 %all-to-all-start = ((s32[8,32,1]{1,2,0:T(1,128)}), s32[8,32,1]{1,2,0:T(1,128)S(1)}, u32[]{:S(2)}, u32[]{:S(2)}) async-start(s32[8,32,1]{1,2,0:T(1,128)} %bitcast.8), calls=%async_computation | async-start | bytes 8192 | tf_op jit(solution)/shard_map/all_to_all | solution.py:109
  20.7 17.6 %collective-permute-start = (f32[3,16,32]{1,0,2:T(4,128)S(1)}, f32[3,16,32]{1,0,2:T(4,128)S(1)}, u32[]{:S(2)}, u32[]{:S(2)}) collective-permute-start(f32[3,16,32]{1,0,2:T(4,128)S(1)} %get-tuple-element.59), channel_id=1, source_target_pairs={{0,4},{4,0},{8,12},{12,8},{16,20},{20,16},{24,28},{28,24},{1,5},{5... | collective-permute-start | bytes 18440 | tf_op jit(solution)/shard_map/ppermute | solution.py:131
  33.5 7.9 %collective-permute-start.1 = (f32[3,16,32]{1,0,2:T(4,128)S(1)}, f32[3,16,32]{1,0,2:T(4,128)S(1)}, u32[]{:S(2)}, u32[]{:S(2)}) collective-permute-start(f32[3,16,32]{1,0,2:T(4,128)S(1)} %get-tuple-element.58), channel_id=1, source_target_pairs={{0,8},{4,12},{8,0},{12,4},{16,24},{20,28},{24,16},{28,20},{1,9},{5... | collective-permute-start | bytes 18440 | tf_op jit(solution)/shard_map/ppermute | solution.py:131
  34.7 6.8 %collective-permute-start.2 = (f32[3,16,32]{1,0,2:T(4,128)S(1)}, f32[3,16,32]{1,0,2:T(4,128)S(1)}, u32[]{:S(2)}, u32[]{:S(2)}) collective-permute-start(f32[3,16,32]{1,0,2:T(4,128)S(1)} %get-tuple-element.57), channel_id=1, source_target_pairs={{0,12},{4,8},{8,4},{12,0},{16,28},{20,24},{24,20},{28,16},{1,13},{... | collective-permute-start | bytes 18440 | tf_op jit(solution)/shard_map/ppermute | solution.py:131
  34.8 6.8 %collective-permute-start.3 = (f32[3,16,32]{1,0,2:T(4,128)S(1)}, f32[3,16,32]{1,0,2:T(4,128)S(1)}, u32[]{:S(2)}, u32[]{:S(2)}) collective-permute-start(f32[3,16,32]{1,0,2:T(4,128)S(1)} %get-tuple-element.56), channel_id=1, source_target_pairs={{0,16},{4,20},{8,24},{12,28},{16,0},{20,4},{24,8},{28,12},{1,17},{... | collective-permute-start | bytes 18440 | tf_op jit(solution)/shard_map/ppermute | solution.py:131
  37.1 10.4 %collective-permute-start.4 = (f32[3,16,32]{1,0,2:T(4,128)S(1)}, f32[3,16,32]{1,0,2:T(4,128)S(1)}, u32[]{:S(2)}, u32[]{:S(2)}) collective-permute-start(f32[3,16,32]{1,0,2:T(4,128)S(1)} %get-tuple-element.55), channel_id=1, source_target_pairs={{0,20},{4,16},{8,28},{12,24},{16,4},{20,0},{24,12},{28,8},{1,21},{... | collective-permute-start | bytes 18440 | tf_op jit(solution)/shard_map/ppermute | solution.py:131
  38.3 9.1 %collective-permute-start.5 = (f32[3,16,32]{1,0,2:T(4,128)S(1)}, f32[3,16,32]{1,0,2:T(4,128)S(1)}, u32[]{:S(2)}, u32[]{:S(2)}) collective-permute-start(f32[3,16,32]{1,0,2:T(4,128)S(1)} %get-tuple-element.54), channel_id=1, source_target_pairs={{0,24},{4,28},{8,16},{12,20},{16,8},{20,12},{24,0},{28,4},{1,25},{... | collective-permute-start | bytes 18440 | tf_op jit(solution)/shard_map/ppermute | solution.py:131
  41.3 6.2 %collective-permute-start.6 = (f32[3,16,32]{1,0,2:T(4,128)S(1)}, f32[3,16,32]{1,0,2:T(4,128)S(1)}, u32[]{:S(2)}, u32[]{:S(2)}) collective-permute-start(f32[3,16,32]{1,0,2:T(4,128)S(1)} %get-tuple-element.53), channel_id=1, source_target_pairs={{0,28},{4,24},{8,20},{12,16},{16,12},{20,8},{24,4},{28,0},{1,29},{... | collective-permute-start | bytes 18440 | tf_op jit(solution)/shard_map/ppermute | solution.py:131
  87.6 8.9 %all-to-all-start.1 = ((f32[8,1,1536]{2,1,0:T(1,128)}), f32[8,1,1536]{2,1,0:T(1,128)S(1)}, u32[]{:S(2)}, u32[]{:S(2)}) async-start(f32[8,1,1536]{2,1,0:T(1,128)} %reshape.339), calls=%async_computation.1 | async-start | bytes 98304 | tf_op jit(solution)/shard_map/all_to_all | solution.py:175
  107.4 10.7 %collective-permute-start.9 = (f32[3,16]{1,0:T(4,128)S(1)}, f32[3,16]{1,0:T(4,128)S(1)}, u32[]{:S(2)}, u32[]{:S(2)}) collective-permute-start(f32[3,16]{1,0:T(4,128)S(1)} %get-tuple-element.85), channel_id=1, source_target_pairs={{4,0},{8,4},{12,8},{16,12},{20,16},{24,20},{28,24},{0,28},{5,1},{9... | collective-permute-start | bytes 584 | tf_op jit(solution)/shard_map/ppermute | solution.py:22
  112.4 7.6 %collective-permute-start.8 = (f32[3,16]{1,0:T(4,128)S(1)}, f32[3,16]{1,0:T(4,128)S(1)}, u32[]{:S(2)}, u32[]{:S(2)}) collective-permute-start(f32[3,16]{1,0:T(4,128)S(1)} %collective-permute-done.7), channel_id=1, source_target_pairs={{0,1},{1,2},{2,3},{4,5},{5,6},{6,7},{8,9},{9,10},{10,11},{12,13},{... | collective-permute-start | bytes 584 | tf_op jit(solution)/shard_map/ppermute | solution.py:30
  123.2 5.1 %collective-permute-start.11 = (f32[3,16]{1,0:T(4,128)S(1)}, f32[3,16]{1,0:T(4,128)S(1)}, u32[]{:S(2)}, u32[]{:S(2)}) collective-permute-start(f32[3,16]{1,0:T(4,128)S(1)} %get-tuple-element.82), channel_id=1, source_target_pairs={{0,4},{4,8},{8,12},{12,16},{16,20},{20,24},{24,28},{28,0},{1,5},{5... | collective-permute-start | bytes 584 | tf_op jit(solution)/shard_map/ppermute | solution.py:19
  123.2 8.2 %collective-permute-start.13 = (f32[3,16]{1,0:T(4,128)S(1)}, f32[3,16]{1,0:T(4,128)S(1)}, u32[]{:S(2)}, u32[]{:S(2)}) collective-permute-start(f32[3,16]{1,0:T(4,128)S(1)} %get-tuple-element.83), channel_id=1, source_target_pairs={{4,0},{8,4},{12,8},{16,12},{20,16},{24,20},{28,24},{0,28},{5,1},{9... | collective-permute-start | bytes 584 | tf_op jit(solution)/shard_map/ppermute | solution.py:22
  138.3 5.1 %collective-permute-start.15 = (f32[3,16,32]{1,0,2:T(4,128)S(1)}, f32[3,16,32]{1,0,2:T(4,128)S(1)}, u32[]{:S(2)}, u32[]{:S(2)}) collective-permute-start(f32[3,16,32]{1,0,2:T(4,128)S(1)} %get-tuple-element.51), channel_id=1, source_target_pairs={{0,4},{4,0},{8,12},{12,8},{16,20},{20,16},{24,28},{28,24},{1,5},{5... | collective-permute-start | bytes 18440 | tf_op jit(solution)/shard_map/ppermute | solution.py:131
  138.6 6.1 %collective-permute-start.16 = (f32[3,16,32]{1,0,2:T(4,128)S(1)}, f32[3,16,32]{1,0,2:T(4,128)S(1)}, u32[]{:S(2)}, u32[]{:S(2)}) collective-permute-start(f32[3,16,32]{1,0,2:T(4,128)S(1)} %get-tuple-element.50), channel_id=1, source_target_pairs={{0,8},{4,12},{8,0},{12,4},{16,24},{20,28},{24,16},{28,20},{1,9},{5... | collective-permute-start | bytes 18440 | tf_op jit(solution)/shard_map/ppermute | solution.py:131
  138.7 9.3 %collective-permute-start.17 = (f32[3,16,32]{1,0,2:T(4,128)S(1)}, f32[3,16,32]{1,0,2:T(4,128)S(1)}, u32[]{:S(2)}, u32[]{:S(2)}) collective-permute-start(f32[3,16,32]{1,0,2:T(4,128)S(1)} %get-tuple-element.49), channel_id=1, source_target_pairs={{0,12},{4,8},{8,4},{12,0},{16,28},{20,24},{24,20},{28,16},{1,13},{... | collective-permute-start | bytes 18440 | tf_op jit(solution)/shard_map/ppermute | solution.py:131
  141.3 9.7 %collective-permute-start.18 = (f32[3,16,32]{1,0,2:T(4,128)S(1)}, f32[3,16,32]{1,0,2:T(4,128)S(1)}, u32[]{:S(2)}, u32[]{:S(2)}) collective-permute-start(f32[3,16,32]{1,0,2:T(4,128)S(1)} %get-tuple-element.48), channel_id=1, source_target_pairs={{0,16},{4,20},{8,24},{12,28},{16,0},{20,4},{24,8},{28,12},{1,17},{... | collective-permute-start | bytes 18440 | tf_op jit(solution)/shard_map/ppermute | solution.py:131
  141.3 11.1 %collective-permute-start.19 = (f32[3,16,32]{1,0,2:T(4,128)S(1)}, f32[3,16,32]{1,0,2:T(4,128)S(1)}, u32[]{:S(2)}, u32[]{:S(2)}) collective-permute-start(f32[3,16,32]{1,0,2:T(4,128)S(1)} %get-tuple-element.47), channel_id=1, source_target_pairs={{0,20},{4,16},{8,28},{12,24},{16,4},{20,0},{24,12},{28,8},{1,21},{... | collective-permute-start | bytes 18440 | tf_op jit(solution)/shard_map/ppermute | solution.py:131
  143.4 9.0 %collective-permute-start.20 = (f32[3,16,32]{1,0,2:T(4,128)S(1)}, f32[3,16,32]{1,0,2:T(4,128)S(1)}, u32[]{:S(2)}, u32[]{:S(2)}) collective-permute-start(f32[3,16,32]{1,0,2:T(4,128)S(1)} %get-tuple-element.46), channel_id=1, source_target_pairs={{0,24},{4,28},{8,16},{12,20},{16,8},{20,12},{24,0},{28,4},{1,25},{... | collective-permute-start | bytes 18440 | tf_op jit(solution)/shard_map/ppermute | solution.py:131
  144.8 7.7 %collective-permute-start.21 = (f32[3,16,32]{1,0,2:T(4,128)S(1)}, f32[3,16,32]{1,0,2:T(4,128)S(1)}, u32[]{:S(2)}, u32[]{:S(2)}) collective-permute-start(f32[3,16,32]{1,0,2:T(4,128)S(1)} %get-tuple-element.45), channel_id=1, source_target_pairs={{0,28},{4,24},{8,20},{12,16},{16,12},{20,8},{24,4},{28,0},{1,29},{... | collective-permute-start | bytes 18440 | tf_op jit(solution)/shard_map/ppermute | solution.py:131
  208.4 10.6 %collective-permute-start.24 = (f32[3,16]{1,0:T(4,128)S(1)}, f32[3,16]{1,0:T(4,128)S(1)}, u32[]{:S(2)}, u32[]{:S(2)}) collective-permute-start(f32[3,16]{1,0:T(4,128)S(1)} %get-tuple-element.81), channel_id=1, source_target_pairs={{4,0},{8,4},{12,8},{16,12},{20,16},{24,20},{28,24},{0,28},{5,1},{9... | collective-permute-start | bytes 584 | tf_op jit(solution)/shard_map/ppermute | solution.py:22
  213.5 7.4 %collective-permute-start.23 = (f32[3,16]{1,0:T(4,128)S(1)}, f32[3,16]{1,0:T(4,128)S(1)}, u32[]{:S(2)}, u32[]{:S(2)}) collective-permute-start(f32[3,16]{1,0:T(4,128)S(1)} %collective-permute-done.22), channel_id=1, source_target_pairs={{0,1},{1,2},{2,3},{4,5},{5,6},{6,7},{8,9},{9,10},{10,11},{12,13},{... | collective-permute-start | bytes 584 | tf_op jit(solution)/shard_map/ppermute | solution.py:30
  224.2 9.0 %collective-permute-start.28 = (f32[3,16]{1,0:T(4,128)S(1)}, f32[3,16]{1,0:T(4,128)S(1)}, u32[]{:S(2)}, u32[]{:S(2)}) collective-permute-start(f32[3,16]{1,0:T(4,128)S(1)} %get-tuple-element.79), channel_id=1, source_target_pairs={{4,0},{8,4},{12,8},{16,12},{20,16},{24,20},{28,24},{0,28},{5,1},{9... | collective-permute-start | bytes 584 | tf_op jit(solution)/shard_map/ppermute | solution.py:22
  229.3 5.8 %collective-permute-start.27 = (f32[3,16]{1,0:T(4,128)S(1)}, f32[3,16]{1,0:T(4,128)S(1)}, u32[]{:S(2)}, u32[]{:S(2)}) collective-permute-start(f32[3,16]{1,0:T(4,128)S(1)} %collective-permute-done.26), channel_id=1, source_target_pairs={{0,1},{1,2},{2,3},{4,5},{5,6},{6,7},{8,9},{9,10},{10,11},{12,13},{... | collective-permute-start | bytes 584 | tf_op jit(solution)/shard_map/ppermute | solution.py:30
  (13 other events, 204.3 us)
